TPU v7x, 32 devices: a whole 2x2x4 slice. The times are simulated.
32 devices in a mesh: dp: 8 (over y, x, core), tensor: 4 (over z).
Axes of the slice: x: 2, y: 2, z: 4, core: 2. Of those that a mesh axis runs over, the one named last changes fastest.
Arguments:
- inputs: bfloat16 [64, 256, 1152], P('dp'), may hold values from -6 to 6
- cotangent: bfloat16 [64, 256, 1152], P('dp'), may hold values from -6 to 6
- counts: int32 [8], P('dp'), may hold values from 1 to 8, as said below
- time_ids: int32 [64], P('dp'), may hold values from 0 to 999
- class_ids: int32 [64], P('dp'), may hold values from 0 to 1000
- time_table: bfloat16 [1000, 1152], replicated, may hold values from -4 to 4
- class_table: bfloat16 [1001, 1152], replicated, may hold values from -4 to 4
- ada_weight: bfloat16 [1152, 6, 1152], P(None, None, 'tensor'), may hold values from -0.1875 to 0.1875
- ada_bias: bfloat16 [6, 1152], P(None, 'tensor'), may hold values from -1.75 to 1.75
- qkv_weight: bfloat16 [1152, 3, 1152], P(None, None, 'tensor'), may hold values from -0.1875 to 0.1875
- qv_bias: bfloat16 [2, 1152], P(None, 'tensor'), may hold values from -1.75 to 1.75
- proj_weight: bfloat16 [1152, 1152], P('tensor'), may hold values from -1.5 to 1.5
- proj_bias: bfloat16 [1152], replicated, may hold values from -1.75 to 1.75
- up_weight: bfloat16 [1152, 4608], P(None, 'tensor'), may hold values from -0.1875 to 0.1875
- up_bias: bfloat16 [4608], P('tensor'), may hold values from -1.75 to 1.75
- down_weight: bfloat16 [4608, 1152], P('tensor'), may hold values from -0.09375 to 0.09375
- down_bias: bfloat16 [1152], replicated, may hold values from -1.75 to 1.75
Outputs:
- outputs: bfloat16 [64, 256, 1152], P('dp')
- grad_inputs: bfloat16 [64, 256, 1152], P('dp')
- grad_time_table: float32 [1000, 1152], replicated
- grad_class_table: float32 [1001, 1152], replicated
- grad_ada_weight: float32 [1152, 6, 1152], P(None, None, 'tensor')
- grad_ada_bias: float32 [6, 1152], P(None, 'tensor')
- grad_qkv_weight: float32 [1152, 3, 1152], P(None, None, 'tensor')
- grad_qv_bias: float32 [2, 1152], P(None, 'tensor')
- grad_proj_weight: float32 [1152, 1152], P('tensor')
- grad_proj_bias: float32 [1152], replicated
- grad_up_weight: float32 [1152, 4608], P(None, 'tensor')
- grad_up_bias: float32 [4608], P('tensor')
- grad_down_weight: float32 [4608, 1152], P('tensor')
- grad_down_bias: float32 [1152], replicated
Inputs may be any that keep to these rules, and one draw needn't show every extreme that they name: Each index of dp holds 8 image slots whose first counts live; at least one index has all 8 live.
All inputs are finite; a program needn't handle non-finite values.
Results may differ from a plain program's by a relative error of at most 0.014.
The roundings to bfloat16 on the way count: a program that leaves them out, or rounds other values in their place, can miss the bound.
Values sent between devices are 32-bit elements; how exact they have to be, the bound alone decides.
No kernel may reach another device: no remote copies, remote signals or barrier semaphores. Data moves between devices by JAX's collectives and lax.ppermute only.
A program may use at most 256 MiB of HBM per device.

v0:
```python
import jax
import jax.numpy as jnp
from jax import lax
from jax.sharding import PartitionSpec as P

HEAD_DIM = 72
EPSILON = 1e-06
GELU_ROOT = 0.7978845608028654
GELU_CUBIC = 0.044715


def norm_parts(values):
    average = jnp.mean(values, axis=-1, keepdims=True)
    centred = values - average
    spread = jnp.mean(centred * centred, axis=-1, keepdims=True)
    inverse = lax.rsqrt(spread + EPSILON)
    return (centred * inverse, inverse)


def norm_back(upstream, normed, inverse):
    first_mean = jnp.mean(upstream, axis=-1, keepdims=True)
    second_mean = jnp.mean(upstream * normed, axis=-1, keepdims=True)
    return inverse * (upstream - first_mean - normed * second_mean)


def gelu_parts(values):
    argument = GELU_ROOT * (values + GELU_CUBIC * values * values * values)
    tangent = jnp.tanh(argument)
    result = 0.5 * values * (1.0 + tangent)
    derivative = 0.5 * (1.0 + tangent) + 0.5 * values * (1.0 - tangent * tangent) * GELU_ROOT * (
        1.0 + 3.0 * GELU_CUBIC * values * values
    )
    return (result, derivative)


def local(
    inputs,
    cotangent,
    counts,
    time_ids,
    class_ids,
    time_table,
    class_table,
    ada_weight,
    ada_bias,
    qkv_weight,
    qv_bias,
    proj_weight,
    proj_bias,
    up_weight,
    up_bias,
    down_weight,
    down_bias,
):
    wide = jnp.float32
    narrow = jnp.bfloat16
    images, length, width = inputs.shape
    local_width = qkv_weight.shape[2]
    heads_here = local_width // HEAD_DIM
    scaling = HEAD_DIM ** (-0.5)
    live = (jnp.arange(images, dtype=jnp.int32) < counts[0]).astype(wide)
    time_levels = jnp.arange(time_table.shape[0], dtype=jnp.int32)
    class_levels = jnp.arange(class_table.shape[0], dtype=jnp.int32)
    time_pick = (time_ids[:, None] == time_levels[None, :]).astype(narrow)
    class_pick = (class_ids[:, None] == class_levels[None, :]).astype(narrow)
    condition = jnp.dot(time_pick, time_table, preferred_element_type=wide) + jnp.dot(
        class_pick, class_table, preferred_element_type=wide
    )
    silu_cond = jax.nn.silu(condition).astype(narrow)
    mod_local = jnp.einsum(
        "gd,dke->gke", silu_cond, ada_weight, preferred_element_type=wide
    ) + ada_bias.astype(wide)
    modulation = lax.all_gather(mod_local, "tensor", axis=2, tiled=True)
    shift_attn = modulation[:, 0, None, :]
    scale_attn = modulation[:, 1, None, :]
    gate_attn = modulation[:, 2, None, :]
    shift_mlp = modulation[:, 3, None, :]
    scale_mlp = modulation[:, 4, None, :]
    gate_mlp = modulation[:, 5, None, :]
    input_wide = inputs.astype(wide)
    normed_attn, inverse_attn = norm_parts(input_wide)
    hidden_attn = (normed_attn * (1.0 + scale_attn) + shift_attn).astype(narrow)
    projected = jnp.einsum("gsd,dke->gske", hidden_attn, qkv_weight, preferred_element_type=wide)
    bias_wide = qv_bias.astype(wide)
    shape_heads = (images, length, heads_here, HEAD_DIM)
    query_heads = (projected[:, :, 0] + bias_wide[0]).astype(narrow).reshape(shape_heads)
    key_heads = projected[:, :, 1].astype(narrow).reshape(shape_heads)
    value_heads = (projected[:, :, 2] + bias_wide[1]).astype(narrow).reshape(shape_heads)
    scores = (
        jnp.einsum("gqhe,gkhe->ghqk", query_heads, key_heads, preferred_element_type=wide) * scaling
    )
    highest = jnp.max(scores, axis=-1, keepdims=True)
    exponent = jnp.exp(scores - highest)
    denominator = jnp.sum(exponent, axis=-1, keepdims=True)
    soft_probs = (exponent / denominator).astype(narrow)
    log_total = highest + jnp.log(denominator)
    heads_out = jnp.einsum("ghqk,gkhe->gqhe", soft_probs, value_heads, preferred_element_type=wide)
    heads_out = heads_out.reshape(images, length, local_width).astype(narrow)
    attn_part = jnp.einsum("gse,ed->gsd", heads_out, proj_weight, preferred_element_type=wide)
    attention = lax.psum(attn_part, "tensor") + proj_bias.astype(wide)
    middle = input_wide + gate_attn * attention
    normed_mlp, inverse_mlp = norm_parts(middle)
    hidden_mlp = (normed_mlp * (1.0 + scale_mlp) + shift_mlp).astype(narrow)
    pre_act = jnp.einsum(
        "gsd,df->gsf", hidden_mlp, up_weight, preferred_element_type=wide
    ) + up_bias.astype(wide)
    gelu_value, gelu_slope = gelu_parts(pre_act)
    activated = gelu_value.astype(narrow)
    mlp_part = jnp.einsum("gsf,fd->gsd", activated, down_weight, preferred_element_type=wide)
    branch = lax.psum(mlp_part, "tensor") + down_bias.astype(wide)
    outputs = ((middle + gate_mlp * branch) * live[:, None, None]).astype(narrow)
    grad_out = cotangent.astype(wide) * live[:, None, None]
    d_gate_mlp = jnp.sum(grad_out * branch, axis=1)
    d_branch = (gate_mlp * grad_out).astype(narrow)
    grad_down_bias = jnp.sum(d_branch, axis=(0, 1), dtype=wide)
    grad_down_weight = jnp.einsum("gsf,gsd->fd", activated, d_branch, preferred_element_type=wide)
    d_activated = jnp.einsum("gsd,fd->gsf", d_branch, down_weight, preferred_element_type=wide)
    d_pre = (d_activated * gelu_slope).astype(narrow)
    grad_up_bias = jnp.sum(d_pre, axis=(0, 1), dtype=wide)
    grad_up_weight = jnp.einsum("gsd,gsf->df", hidden_mlp, d_pre, preferred_element_type=wide)
    grad_down_weight, grad_down_bias, grad_up_weight, grad_up_bias = lax.psum(
        (grad_down_weight, grad_down_bias, grad_up_weight, grad_up_bias), "dp"
    )
    d_mlp_part = jnp.einsum("gsf,df->gsd", d_pre, up_weight, preferred_element_type=wide)
    d_hidden_mlp = lax.psum(d_mlp_part, "tensor")
    d_shift_mlp = jnp.sum(d_hidden_mlp, axis=1)
    d_scale_mlp = jnp.sum(d_hidden_mlp * normed_mlp, axis=1)
    d_middle = grad_out + norm_back(d_hidden_mlp * (1.0 + scale_mlp), normed_mlp, inverse_mlp)
    d_gate_attn = jnp.sum(d_middle * attention, axis=1)
    d_attention = (gate_attn * d_middle).astype(narrow)
    grad_proj_bias = jnp.sum(d_attention, axis=(0, 1), dtype=wide)
    grad_proj_weight = jnp.einsum(
        "gse,gsd->ed", heads_out, d_attention, preferred_element_type=wide
    )
    d_heads = jnp.einsum("gsd,ed->gse", d_attention, proj_weight, preferred_element_type=wide)
    d_heads = d_heads.astype(narrow).reshape(shape_heads)
    scores_again = (
        jnp.einsum("gqhe,gkhe->ghqk", query_heads, key_heads, preferred_element_type=wide) * scaling
    )
    probs_again = jnp.exp(scores_again - log_total)
    d_value = jnp.einsum(
        "ghqk,gqhe->gkhe", probs_again.astype(narrow), d_heads, preferred_element_type=wide
    )
    d_value = d_value.astype(narrow)
    d_probs = jnp.einsum("gqhe,gkhe->ghqk", d_heads, value_heads, preferred_element_type=wide)
    row_inner = jnp.sum(probs_again * d_probs, axis=-1, keepdims=True)
    d_scores = (probs_again * (d_probs - row_inner)).astype(narrow)
    d_query = (
        jnp.einsum("ghqk,gkhe->gqhe", d_scores, key_heads, preferred_element_type=wide) * scaling
    ).astype(narrow)
    d_key = (
        jnp.einsum("ghqk,gqhe->gkhe", d_scores, query_heads, preferred_element_type=wide) * scaling
    ).astype(narrow)
    d_projected = jnp.stack([d_query, d_key, d_value], axis=2).reshape(
        images, length, 3, local_width
    )
    grad_qv_bias = jnp.stack(
        [
            jnp.sum(d_query, axis=(0, 1), dtype=wide).reshape(local_width),
            jnp.sum(d_value, axis=(0, 1), dtype=wide).reshape(local_width),
        ],
        axis=0,
    )
    grad_qkv_weight = jnp.einsum(
        "gsd,gske->dke", hidden_attn, d_projected, preferred_element_type=wide
    )
    d_attn_part = jnp.einsum("gske,dke->gsd", d_projected, qkv_weight, preferred_element_type=wide)
    d_hidden_attn = lax.psum(d_attn_part, "tensor")
    d_shift_attn = jnp.sum(d_hidden_attn, axis=1)
    d_scale_attn = jnp.sum(d_hidden_attn * normed_attn, axis=1)
    grad_inputs = (
        d_middle + norm_back(d_hidden_attn * (1.0 + scale_attn), normed_attn, inverse_attn)
    ).astype(narrow)
    d_modulation = jnp.stack(
        [d_shift_attn, d_scale_attn, d_gate_attn, d_shift_mlp, d_scale_mlp, d_gate_mlp], axis=1
    ).astype(narrow)
    start_column = lax.axis_index("tensor") * local_width
    d_mod_local = lax.dynamic_slice_in_dim(d_modulation, start_column, local_width, 2)
    grad_ada_weight = jnp.einsum("gd,gke->dke", silu_cond, d_mod_local, preferred_element_type=wide)
    grad_ada_bias = jnp.sum(d_mod_local, axis=0, dtype=wide)
    (
        grad_qkv_weight,
        grad_qv_bias,
        grad_proj_weight,
        grad_proj_bias,
        grad_ada_weight,
        grad_ada_bias,
    ) = lax.psum(
        (
            grad_qkv_weight,
            grad_qv_bias,
            grad_proj_weight,
            grad_proj_bias,
            grad_ada_weight,
            grad_ada_bias,
        ),
        "dp",
    )
    sigmoid_cond = jax.nn.sigmoid(condition)
    d_condition = jnp.einsum("gke,dke->gd", d_mod_local, ada_weight, preferred_element_type=wide)
    d_condition = d_condition * sigmoid_cond * (1.0 + condition * (1.0 - sigmoid_cond))
    exact = lax.Precision.HIGHEST
    grad_time_table = jnp.dot(time_pick.astype(wide).T, d_condition, precision=exact)
    grad_class_table = jnp.dot(class_pick.astype(wide).T, d_condition, precision=exact)
    grad_time_table, grad_class_table = lax.psum(
        (grad_time_table, grad_class_table), ("dp", "tensor")
    )
    return (
        outputs,
        grad_inputs,
        grad_time_table,
        grad_class_table,
        grad_ada_weight,
        grad_ada_bias,
        grad_qkv_weight,
        grad_qv_bias,
        grad_proj_weight,
        grad_proj_bias,
        grad_up_weight,
        grad_up_bias,
        grad_down_weight,
        grad_down_bias,
    )


def solution(mesh):
    in_specs = (
        P("dp", None, None),
        P("dp", None, None),
        P("dp"),
        P("dp"),
        P("dp"),
        P(),
        P(),
        P(None, None, "tensor"),
        P(None, "tensor"),
        P(None, None, "tensor"),
        P(None, "tensor"),
        P("tensor", None),
        P(),
        P(None, "tensor"),
        P("tensor"),
        P("tensor", None),
        P(),
    )
    out_specs = (
        P("dp", None, None),
        P("dp", None, None),
        P(),
        P(),
        P(None, None, "tensor"),
        P(None, "tensor"),
        P(None, None, "tensor"),
        P(None, "tensor"),
        P("tensor", None),
        P(),
        P(None, "tensor"),
        P("tensor"),
        P("tensor", None),
        P(),
    )
    return jax.shard_map(local, mesh=mesh, in_specs=in_specs, out_specs=out_specs, check_vma=False)
```

profile of v0, /device:TPU:0, one launch (start us, length us, event | category | flops | bytes accessed | tf_op | source)
XLA Modules:
  0.0 2098.7 jit_solution(2705256795855632784)
XLA Ops:
  10.5 4.5 fusion.14
  19.4 91.1 %all_gather.3 = f32[8,6,1152]{1,0,2:T(8,128)} all-gather(f32[8,6,288]{1,0,2:T(8,128)} %copy.58), channel_id=1, replica_groups=mesh['dp'=8,'tensor'=4] {'tensor'}, dimensions={2}, use_global_device_ids=true | all-gather | bytes 276480 | tf_op jit(solution)/shard_map/all_gather | solution.py:73
  110.5 22.1 %fusion.73 = (f32[8,1,1152]{1,0,2:T(8,128)}, f32[8,1,1152]{1,0,2:T(8,128)}, f32[8,1,1152]{1,0,2:T(8,128)}, f32[8,1,1152]{1,0,2:T(8,128)}, f32[8,1,1152]{1,0,2:T(8,128)}, /*index=5*/f32[8,1,1152]{1,0,2:T(8,128)}) fusion(f32[8,6,1152]{1,0,2:T(8,128)} %all_gather.3), kind=kLoop, calls=%fused_computation.140 | loop fusion | bytes 442368 | tf_op jit(solution)/shard_map/slice | solution.py:79
  139.3 7.8 fusion.40
  159.6 5.4 fusion.49
  180.0 310.3 %all-reduce.10.cloned.1.call-done = f32[8,256,1152]{2,1,0:T(8,128)} async-done(((f32[8,256,1152]{2,1,0:T(8,128)}), f32[8,256,1152]{2,1,0:T(8,128)}) %all-reduce.10.cloned.1.call-update) | async-done | bytes 9437200 | tf_op jit(solution)/shard_map/psum | solution.py:100
  490.3 10.4 fusion.71
  500.7 4.9 multiply_reduce_fusion.4
  507.1 9.6 fusion.35
  516.7 12.8 convert_reduce_fusion.2
  531.8 9.6 fusion.33
  542.2 13.1 fusion.31
  555.3 309.9 %all-reduce.12.cloned.1.call-done = f32[8,256,1152]{2,1,0:T(8,128)} async-done(((f32[8,256,1152]{2,1,0:T(8,128)}), f32[8,256,1152]{2,1,0:T(8,128)}) %all-reduce.12.cloned.1.call-update) | async-done | bytes 9437200 | tf_op jit(solution)/shard_map/psum | solution.py:125
  865.2 8.5 multiply_reduce_fusion.1
  874.4 11.4 convert_reduce_fusion.3
  900.4 7.9 convolution_bitcast_fusion.2
  909.1 16.6 convolution_bitcast_fusion
  925.7 611.2 %all-reduce.18.cloned.1.call-done = (f32[8,256,1152]{2,1,0:T(8,128)}, f32[8,256,1152]{2,1,0:T(8,128)}) async-done(((f32[8,256,1152]{2,1,0:T(8,128)}, f32[8,256,1152]{2,1,0:T(8,128)}), (f32[8,256,1152]{2,1,0:T(8,128)}, f32[8,256,1152]{2,1,0:T(8,128)})) %all-reduce.18.cloned.1.call-update) | async-done | bytes 18874384 | tf_op jit(solution)/shard_map/psum | solution.py:110
  1537.0 8.8 fusion.13
  1545.9 13.2 convert_reduce_fusion.1
  1559.3 9.1 multiply_reduce_fusion.2
  1569.2 4.4 fusion.54
  1573.6 4.3 fusion.53
  1578.4 15.1 convolution_bitcast_fusion.1
  1593.5 5.3 convolution_bitcast_fusion.4
  1598.8 9.8 convolution_bitcast_fusion.3
  1608.6 4.7 fusion.56
  1614.0 24.1 %all-reduce.1 = (f32[6,288]{1,0:T(8,128)}, f32[2,288]{1,0:T(2,128)}, f32[1152]{0:T(1024)}, f32[1152]{0:T(1024)}, f32[1152]{0:T(1024)}) all-reduce(f32[6,288]{1,0:T(8,128)S(1)} %convert_reduce_fusion.6, f32[2,288]{1,0:T(2,128)S(1)} %pad_maximum_fusion.3, f32[1152]{0:T(1024)S(1)} %copy-done.42, ...), channel_id=1, replica_groups=mesh['dp'=8,'tensor'=4] {'dp'}, use_global_device_ids=true, to_apply=%region_25.26 | all-reduce | flops 5760 | bytes 46080 | tf_op jit(solution)/shard_map/psum | solution.py:188
  1638.2 128.6 %all-reduce.14.cloned.1.call-done = (f32[1000,1152]{1,0:T(8,128)}, f32[1001,1152]{1,0:T(8,128)}) async-done(((f32[1000,1152]{1,0:T(8,128)}, f32[1001,1152]{1,0:T(8,128)}), (f32[1000,1152]{1,0:T(8,128)}, f32[1001,1152]{1,0:T(8,128)})) %all-reduce.14.cloned.1.call-update) | async-done | bytes 9220624 | tf_op jit(solution)/shard_map/psum | solution.py:205
  1766.7 300.5 %all-reduce.16.cloned.1.call-done = (f32[1152,6,288]{0,2,1:T(8,128)}, f32[1152,3,288]{0,2,1:T(8,128)}, f32[288,1152]{1,0:T(8,128)}, f32[1152,1152]{1,0:T(8,128)}, f32[1152,1152]{1,0:T(8,128)}) async-done(((f32[1152,6,288]{0,2,1:T(8,128)}, f32[1152,3,288]{0,2,1:T(8,128)}, f32[288,1152]{1,0:T(8,128)}, f32[1152,1152]{1,0:T(8,128)}, f32[1152,1152]{1,0:T(8,128)}), (f32[1152,6,288]{0,2,1:T(8,128)}, ...) | async-done | bytes 23887888 | tf_op jit(solution)/shard_map/psum | solution.py:188
  2067.2 5.1 copy.107
  2076.8 4.0 copy.109
  (231 shorter events, 78.9 us)
Async XLA Ops:
  7.2 509.5 %copy-start = (bf16[1152,1152]{1,0:T(8,128)(2,1)S(1)}, bf16[1152,1152]{1,0:T(8,128)(2,1)}, u32[]{:S(2)}) copy-start(bf16[1152,1152]{1,0:T(8,128)(2,1)} %param.32) | copy-start | bytes 7962628
  7.2 483.1 %all-reduce.10.cloned.1.call-start = ((), (), s32[]{:S(2)}) async-start(), calls=%async_computation | async-start | bytes 18874368 | tf_op jit(solution)/shard_map/psum | solution.py:100
  7.3 9.4 copy-start.6
  10.5 128.8 %copy-start.32 = (f32[8,256]{1,0:T(8,128)}, f32[8,256]{1,0:T(8,128)S(1)}, u32[]{:S(2)}) copy-start(f32[8,256]{1,0:T(8,128)S(1)} %broadcast_multiply_fusion.5) | copy-start | bytes 24580
  15.0 124.3 %copy-start.34 = (f32[8,256]{1,0:T(8,128)}, f32[8,256]{1,0:T(8,128)S(1)}, u32[]{:S(2)}) copy-start(f32[8,256]{1,0:T(8,128)S(1)} %add_rsqrt_fusion.1) | copy-start | bytes 24580
  135.9 11.2 copy-start.38
  165.0 700.2 %all-reduce.12.cloned.1.call-start = ((), (), s32[]{:S(2)}) async-start(), calls=%async_computation.1 | async-start | bytes 18874368 | tf_op jit(solution)/shard_map/psum | solution.py:125
  165.7 324.6 %copy-start.36 = (f32[1152]{0:T(1024)}, f32[1152]{0:T(1024)S(1)}, u32[]{:S(2)}) copy-start(f32[1152]{0:T(1024)S(1)} %convert_element_type.142) | copy-start | bytes 13828
  180.0 336.7 %copy-start.54 = (f32[8]{0:T(128)}, f32[8]{0:T(128)S(1)}, u32[]{:S(2)}) copy-start(f32[8]{0:T(128)S(1)} %compare_convert_fusion) | copy-start | bytes 100
  490.3 15.3 copy-start.57
  500.7 15.9 slice-start.10
  507.1 9.6 slice-start.11
  541.5 995.5 %all-reduce.18.cloned.1.call-start = ((), (), s32[]{:S(2)}) async-start(), calls=%async_computation.4 | async-start | bytes 37748736 | tf_op jit(solution)/shard_map/psum | solution.py:110
  555.3 318.4 %copy-start.55 = (f32[8]{0:T(128)S(1)}, f32[8]{0:T(128)}, u32[]{:S(2)}) copy-start(f32[8]{0:T(128)} %copy-done.54) | copy-start | bytes 100
  908.4 858.3 %all-reduce.14.cloned.1.call-start = ((), (), s32[]{:S(2)}) async-start(), calls=%async_computation.2 | async-start | bytes 18505728 | tf_op jit(solution)/shard_map/psum | solution.py:205
  909.1 627.9 %copy-start.29 = (f32[8,1152]{1,0:T(8,128)S(1)}, f32[8,1152]{1,0:T(8,128)}, u32[]{:S(2)}) copy-start(f32[8,1152]{1,0:T(8,128)} %copy-done.28) | copy-start | bytes 110596
  909.1 627.9 %copy-start.33 = (f32[8,256]{1,0:T(8,128)S(1)}, f32[8,256]{1,0:T(8,128)}, u32[]{:S(2)}) copy-start(f32[8,256]{1,0:T(8,128)} %copy-done.32) | copy-start | bytes 24580
  909.1 627.9 %copy-start.35 = (f32[8,256]{1,0:T(8,128)S(1)}, f32[8,256]{1,0:T(8,128)}, u32[]{:S(2)}) copy-start(f32[8,256]{1,0:T(8,128)} %copy-done.34) | copy-start | bytes 24580
  1537.0 22.2 %slice-start.2 = ((s8[4718592]{0:T(1024)(128)(4,1)}), s8[4194304]{0:T(1024)(128)(4,1)S(1)}, s32[]{:S(2)}) async-start(s8[4718592]{0:T(1024)(128)(4,1)} %bitcast.124), calls=%async_computation.7 | async-start | bytes 8388608
  1537.0 22.2 %slice-start.4 = ((s8[9437184]{0:T(1024)(128)(4,1)}), s8[4194304]{0:T(1024)(128)(4,1)S(1)}, s32[]{:S(2)}) async-start(s8[9437184]{0:T(1024)(128)(4,1)} %bitcast.126), calls=%async_computation.9 | async-start | bytes 8388608
  1537.0 22.2 %slice-start.5 = ((s8[9437184]{0:T(1024)(128)(4,1)}), s8[4194304]{0:T(1024)(128)(4,1)S(1)}, s32[]{:S(2)}) async-start(s8[9437184]{0:T(1024)(128)(4,1)} %bitcast.126), calls=%async_computation.10 | async-start | bytes 8388608
  1537.0 22.2 %slice-start.7 = ((s8[9437184]{0:T(1024)(128)(4,1)}), s8[4194304]{0:T(1024)(128)(4,1)S(1)}, s32[]{:S(2)}) async-start(s8[9437184]{0:T(1024)(128)(4,1)} %bitcast.128), calls=%async_computation.12 | async-start | bytes 8388608
  1537.0 22.2 %slice-start.8 = ((s8[9437184]{0:T(1024)(128)(4,1)}), s8[4194304]{0:T(1024)(128)(4,1)S(1)}, s32[]{:S(2)}) async-start(s8[9437184]{0:T(1024)(128)(4,1)} %bitcast.128), calls=%async_computation.13 | async-start | bytes 8388608
  1545.9 13.3 slice-start.3
  1545.9 13.3 slice-start.6
  1545.9 13.3 slice-start.9
  1545.9 13.3 copy-start.37
  1559.3 9.9 copy-start.51
  1569.2 9.2 copy-start.41
  1577.9 15.6 copy-start.18
  1577.9 489.3 %all-reduce.16.cloned.1.call-start = ((), (), s32[]{:S(2)}) async-start(), calls=%async_computation.3 | async-start | bytes 47775744 | tf_op jit(solution)/shard_map/psum | solution.py:188
  2072.3 12.5 slice-start.16
  (51 other events, 257.0 us)
Sparse Core Ops, SparseCore 0:
  165.1 325.1 all-reduce.9
  541.6 323.5 all-reduce.11
  908.5 628.3 all-reduce.17
  1578.0 188.6 all-reduce.13
  1772.5 294.6 all-reduce.15
where the time goes:
time: 2100 us
  waiting for transfers between devices  1660 us (79%)
  matrix products  144 us (7%)
  blocking collectives  115 us (5%)
  local copies, waits for them, and re-layouts  84.7 us (4%)
  other arithmetic  78.3 us (4%)
    psum x1, waiting for transfers between devices, local(): branch = lax.psum(mlp_part, 'tensor') + down_bias.astype(wide)  611 us
    psum x1, waiting for transfers between devices, local(): attention = lax.psum(attn_part, 'tensor') + proj_bias.astype(wide)  310 us
    psum x1, waiting for transfers between devices, local(): d_hidden_mlp = lax.psum(d_mlp_part, 'tensor')  310 us
    psum x1, waiting for transfers between devices, local(): lax.psum((grad_qkv_weight, grad_qv_bias, grad_proj_weight, grad_proj_bias...  300 us
    psum x1, waiting for transfers between devices, local(): lax.psum((grad_time_table, grad_class_table), ('dp', 'tensor'))  129 us
    all_gather x1, blocking collectives, local(): modulation = lax.all_gather(mod_local, 'tensor', axis=2, tiled=True)  91.1 us
    unnamed x174, local copies, waits for them, and re-layouts  57 us
  transfers between devices with their start and end apart: 5, of which 5 were waited for; matrix products, arithmetic and copies ran while one was open for 4% of the time, Pallas kernels for 0%

commit v1 on v0

--- a/solution.py
+++ b/solution.py
@@ -70,7 +70,9 @@
     mod_local = jnp.einsum(
         "gd,dke->gke", silu_cond, ada_weight, preferred_element_type=wide
     ) + ada_bias.astype(wide)
-    modulation = lax.all_gather(mod_local, "tensor", axis=2, tiled=True)
+    modulation = jnp.concatenate(
+        lax.all_to_all(jnp.stack([mod_local] * lax.axis_size("tensor")), "tensor", 0, 0), axis=2
+    )
     shift_attn = modulation[:, 0, None, :]
     scale_attn = modulation[:, 1, None, :]
     gate_attn = modulation[:, 2, None, :]

time: 2100 us -> 2000 us (0.952)
  blocking collectives: 115 us -> 24.2 us
  local copies, waits for them, and re-layouts: 84.7 us -> 39.4 us
    all_gather x1 -> x0, blocking collectives: 91.1 us -> none  [local(): modulation = lax.all_gather(mod_local, 'tensor', axis=2, tiled=True)]
    slice x1 -> x0, local copies, waits for them, and re-layouts: 22.1 us -> none  [local(): gate_mlp = modulation[:, 5, None, :]]
    unnamed x174 -> x156, local copies, waits for them, and re-layouts: 57 us -> 37.4 us
  transfers between devices with their start and end apart: 5 -> 6, of which waited for: 5 -> 6; matrix products, arithmetic and copies ran while one was open for 4% -> 4% of each run, Pallas kernels for 0% -> 0%
where the time goes in v1:
time: 2000 us; the launch traced here: 1990 us
  waiting for transfers between devices  1680 us (84%)
  matrix products  146 us (7%)
  other arithmetic  79.2 us (4%)
  local copies, waits for them, and re-layouts  39.4 us (2%)
  blocking collectives  24.2 us (1%)
    psum x1, waiting for transfers between devices, local(): branch = lax.psum(mlp_part, 'tensor') + down_bias.astype(wide)  611 us
    psum x1, waiting for transfers between devices, local(): attention = lax.psum(attn_part, 'tensor') + proj_bias.astype(wide)  323 us
    psum x1, waiting for transfers between devices, local(): d_hidden_mlp = lax.psum(d_mlp_part, 'tensor')  310 us
    psum x1, waiting for transfers between devices, local(): lax.psum((grad_qkv_weight, grad_qv_bias, grad_proj_weight, grad_proj_bias...  300 us
    psum x1, waiting for transfers between devices, local(): lax.psum((grad_time_table, grad_class_table), ('dp', 'tensor'))  129 us
  transfers between devices with their start and end apart: 6, of which 6 were waited for; matrix products, arithmetic and copies ran while one was open for 4% of the time, Pallas kernels for 0%

profile of v1, /device:TPU:0, one launch (start us, length us, event | category | flops | bytes accessed | tf_op | source)
XLA Modules:
  0.0 1988.1 jit_solution(2790765325607285916)
XLA Ops:
  12.9 3.5 convolution_add_fusion.1
  17.2 6.3 all-to-all-start
  26.6 3.7 fusion.14
  34.7 7.8 fusion.40
  50.8 5.2 fusion.49
  57.2 322.6 %all-reduce.10.cloned.1.call-done = f32[8,256,1152]{2,1,0:T(8,128)} async-done(((f32[8,256,1152]{2,1,0:T(8,128)}), f32[8,256,1152]{2,1,0:T(8,128)}) %all-reduce.10.cloned.1.call-update) | async-done | bytes 9437200 | tf_op jit(solution)/shard_map/psum | solution.py:102
  379.9 10.4 fusion.73
  390.3 4.9 multiply_reduce_fusion.4
  396.7 9.6 fusion.35
  406.3 12.8 convert_reduce_fusion.2
  421.3 9.2 fusion.33
  430.8 13.1 fusion.31
  444.0 310.4 %all-reduce.12.cloned.1.call-done = f32[8,256,1152]{2,1,0:T(8,128)} async-done(((f32[8,256,1152]{2,1,0:T(8,128)}), f32[8,256,1152]{2,1,0:T(8,128)}) %all-reduce.12.cloned.1.call-update) | async-done | bytes 9437200 | tf_op jit(solution)/shard_map/psum | solution.py:127
  754.4 8.5 multiply_reduce_fusion.1
  763.5 11.4 convert_reduce_fusion.3
  789.6 7.9 convolution_bitcast_fusion.2
  798.3 16.6 convolution_bitcast_fusion
  814.9 611.2 %all-reduce.18.cloned.1.call-done = (f32[8,256,1152]{2,1,0:T(8,128)}, f32[8,256,1152]{2,1,0:T(8,128)}) async-done(((f32[8,256,1152]{2,1,0:T(8,128)}, f32[8,256,1152]{2,1,0:T(8,128)}), (f32[8,256,1152]{2,1,0:T(8,128)}, f32[8,256,1152]{2,1,0:T(8,128)})) %all-reduce.18.cloned.1.call-update) | async-done | bytes 18874384 | tf_op jit(solution)/shard_map/psum | solution.py:112
  1426.2 9.1 fusion.13
  1435.3 13.2 convert_reduce_fusion.1
  1448.7 9.1 multiply_reduce_fusion.2
  1458.6 4.4 fusion.56
  1463.0 4.3 fusion.55
  1467.6 15.1 convolution_bitcast_fusion.1
  1482.7 5.3 convolution_bitcast_fusion.4
  1488.0 9.9 convolution_bitcast_fusion.3
  1497.8 4.7 fusion.58
  1503.2 24.2 %all-reduce.1 = (f32[6,288]{1,0:T(8,128)}, f32[2,288]{1,0:T(2,128)}, f32[1152]{0:T(1024)}, f32[1152]{0:T(1024)}, f32[1152]{0:T(1024)}) all-reduce(f32[6,288]{1,0:T(8,128)S(1)} %convert_reduce_fusion.6, f32[2,288]{1,0:T(2,128)S(1)} %pad_maximum_fusion.3, f32[1152]{0:T(1024)S(1)} %copy-done.39, ...), channel_id=1, replica_groups=mesh['dp'=8,'tensor'=4] {'dp'}, use_global_device_ids=true, to_apply=%region_25.26 | all-reduce | flops 5760 | bytes 46080 | tf_op jit(solution)/shard_map/psum | solution.py:190
  1527.5 128.7 %all-reduce.14.cloned.1.call-done = (f32[1000,1152]{1,0:T(8,128)}, f32[1001,1152]{1,0:T(8,128)}) async-done(((f32[1000,1152]{1,0:T(8,128)}, f32[1001,1152]{1,0:T(8,128)}), (f32[1000,1152]{1,0:T(8,128)}, f32[1001,1152]{1,0:T(8,128)})) %all-reduce.14.cloned.1.call-update) | async-done | bytes 9220624 | tf_op jit(solution)/shard_map/psum | solution.py:207
  1656.1 300.5 %all-reduce.16.cloned.1.call-done = (f32[1152,6,288]{0,2,1:T(8,128)}, f32[1152,3,288]{0,2,1:T(8,128)}, f32[288,1152]{1,0:T(8,128)}, f32[1152,1152]{1,0:T(8,128)}, f32[1152,1152]{1,0:T(8,128)}) async-done(((f32[1152,6,288]{0,2,1:T(8,128)}, f32[1152,3,288]{0,2,1:T(8,128)}, f32[288,1152]{1,0:T(8,128)}, f32[1152,1152]{1,0:T(8,128)}, f32[1152,1152]{1,0:T(8,128)}), (f32[1152,6,288]{0,2,1:T(8,128)}, ...) | async-done | bytes 23887888 | tf_op jit(solution)/shard_map/psum | solution.py:190
  1956.6 5.1 copy.88
  1966.2 4.0 copy.90
  (214 shorter events, 59.8 us)
Async XLA Ops:
  7.2 399.1 %copy-start = (bf16[1152,1152]{1,0:T(8,128)(2,1)S(1)}, bf16[1152,1152]{1,0:T(8,128)(2,1)}, u32[]{:S(2)}) copy-start(bf16[1152,1152]{1,0:T(8,128)(2,1)} %param.32) | copy-start | bytes 7962628
  7.2 16.3 copy-start.50
  17.2 16.0 all-to-all-start
  23.5 356.4 %all-reduce.10.cloned.1.call-start = ((), (), s32[]{:S(2)}) async-start(), calls=%async_computation.1 | async-start | bytes 18874368 | tf_op jit(solution)/shard_map/psum | solution.py:102
  26.6 15.9 copy-start.29
  30.4 17.1 copy-start.41
  30.5 12.0 copy-start.31
  56.0 698.4 %all-reduce.12.cloned.1.call-start = ((), (), s32[]{:S(2)}) async-start(), calls=%async_computation.2 | async-start | bytes 18874368 | tf_op jit(solution)/shard_map/psum | solution.py:127
  57.2 333.1 %copy-start.33 = (f32[1152]{0:T(1024)}, f32[1152]{0:T(1024)S(1)}, u32[]{:S(2)}) copy-start(f32[1152]{0:T(1024)S(1)} %convert_element_type.142) | copy-start | bytes 13828
  57.2 349.0 %copy-start.48 = (f32[8]{0:T(128)}, f32[8]{0:T(128)S(1)}, u32[]{:S(2)}) copy-start(f32[8]{0:T(128)S(1)} %compare_convert_fusion) | copy-start | bytes 100
  379.9 15.4 copy-start.51
  390.3 15.9 slice-start.10
  396.7 9.6 slice-start.11
  430.6 995.5 %all-reduce.18.cloned.1.call-start = ((), (), s32[]{:S(2)}) async-start(), calls=%async_computation.5 | async-start | bytes 37748736 | tf_op jit(solution)/shard_map/psum | solution.py:112
  444.0 318.9 %copy-start.49 = (f32[8]{0:T(128)S(1)}, f32[8]{0:T(128)}, u32[]{:S(2)}) copy-start(f32[8]{0:T(128)} %copy-done.48) | copy-start | bytes 100
  797.6 858.5 %all-reduce.14.cloned.1.call-start = ((), (), s32[]{:S(2)}) async-start(), calls=%async_computation.3 | async-start | bytes 18505728 | tf_op jit(solution)/shard_map/psum | solution.py:207
  798.3 627.9 %copy-start.28 = (f32[8,1152]{1,0:T(8,128)S(1)}, f32[8,1152]{1,0:T(8,128)}, u32[]{:S(2)}) copy-start(f32[8,1152]{1,0:T(8,128)} %copy-done.27) | copy-start | bytes 110596
  798.3 627.9 %copy-start.30 = (f32[8,256]{1,0:T(8,128)S(1)}, f32[8,256]{1,0:T(8,128)}, u32[]{:S(2)}) copy-start(f32[8,256]{1,0:T(8,128)} %copy-done.29) | copy-start | bytes 24580
  798.3 627.9 %copy-start.32 = (f32[8,256]{1,0:T(8,128)S(1)}, f32[8,256]{1,0:T(8,128)}, u32[]{:S(2)}) copy-start(f32[8,256]{1,0:T(8,128)} %copy-done.31) | copy-start | bytes 24580
  1426.1 22.4 %slice-start.2 = ((s8[4718592]{0:T(1024)(128)(4,1)}), s8[4194304]{0:T(1024)(128)(4,1)S(1)}, s32[]{:S(2)}) async-start(s8[4718592]{0:T(1024)(128)(4,1)} %bitcast.131), calls=%async_computation.8 | async-start | bytes 8388608
  1426.1 22.4 %slice-start.4 = ((s8[9437184]{0:T(1024)(128)(4,1)}), s8[4194304]{0:T(1024)(128)(4,1)S(1)}, s32[]{:S(2)}) async-start(s8[9437184]{0:T(1024)(128)(4,1)} %bitcast.133), calls=%async_computation.10 | async-start | bytes 8388608
  1426.2 22.4 %slice-start.5 = ((s8[9437184]{0:T(1024)(128)(4,1)}), s8[4194304]{0:T(1024)(128)(4,1)S(1)}, s32[]{:S(2)}) async-start(s8[9437184]{0:T(1024)(128)(4,1)} %bitcast.133), calls=%async_computation.11 | async-start | bytes 8388608
  1426.2 22.4 %slice-start.7 = ((s8[9437184]{0:T(1024)(128)(4,1)}), s8[4194304]{0:T(1024)(128)(4,1)S(1)}, s32[]{:S(2)}) async-start(s8[9437184]{0:T(1024)(128)(4,1)} %bitcast.135), calls=%async_computation.13 | async-start | bytes 8388608
  1426.2 22.4 %slice-start.8 = ((s8[9437184]{0:T(1024)(128)(4,1)}), s8[4194304]{0:T(1024)(128)(4,1)S(1)}, s32[]{:S(2)}) async-start(s8[9437184]{0:T(1024)(128)(4,1)} %bitcast.135), calls=%async_computation.14 | async-start | bytes 8388608
  1435.3 13.3 slice-start.3
  1435.3 13.3 slice-start.6
  1435.3 13.3 slice-start.9
  1435.3 13.3 copy-start.34
  1448.7 9.9 copy-start.46
  1467.3 15.3 copy-start.17
  1467.3 489.3 %all-reduce.16.cloned.1.call-start = ((), (), s32[]{:S(2)}) async-start(), calls=%async_computation.4 | async-start | bytes 47775744 | tf_op jit(solution)/shard_map/psum | solution.py:190
  1961.7 12.5 slice-start.16
  (46 other events, 211.8 us)
Sparse Core Ops, SparseCore 0:
  56.1 323.7 all-reduce.9
  430.7 323.6 all-reduce.11
  797.7 628.3 all-reduce.17
  1467.4 188.6 all-reduce.13
  1661.9 294.6 all-reduce.15
